TPU v7x, 32 devices: a whole 2x2x4 slice. The times are simulated.
32 devices in a mesh: dp: 16 (over z, y, x), rep: 2 (over core).
Axes of the slice: x: 2, y: 2, z: 4, core: 2. Of those that a mesh axis runs over, the one named last changes fastest.
Arguments:
- hidden_old: bfloat16 [8192, 6144], P(('dp', 'rep')), may hold values from -400 to 400
- cotangent: bfloat16 [8192, 128], P(('dp', 'rep')), may hold values from -0.15625 to 0.15625
- gain_old: float32 [6144], replicated, may hold values from 0.1 to 1.9
- old_bounds: int32 [17], replicated, may hold values from 0 to 6144, as said below
- new_bounds: int32 [17], replicated, may hold values from 0 to 8192, as said below
- source_map: int32 [8192], replicated, may hold values from 0 to 6143, as said below
- weight_old: bfloat16 [8192, 128], P('dp'), may hold values from -0.078125 to 0.078125
- moment_first: float32 [8192, 128], P('dp'), may hold values from -6 to 6
- moment_second: float32 [8192, 128], P('dp'), may hold values from 0.25 to 4
Outputs:
- projected: bfloat16 [8192, 128], P(('dp', 'rep'))
- gain_grad: float32 [8192], replicated
- first_next: float32 [10240, 128], P('dp')
- second_next: float32 [10240, 128], P('dp')
- adam_step: float32 [10240, 128], P('dp')
Inputs may be any that keep to these rules, and one draw needn't show every extreme that they name: old_bounds[0] = 0, old_bounds[16] = 6144; device p holds old units old_bounds[p] to old_bounds[p+1] - 1, between 256 and 512 of them, exactly 512 on some device. new_bounds[0] = 0, new_bounds[16] = 8192; device q holds new units new_bounds[q] to new_bounds[q+1] - 1, between 384 and 640 of them, exactly 640 on some device. `source_map`: the s-th new unit of a device (counted from its first) copies an old unit held by old device (s + c) mod 16, with an offset c of that new device; so at most 40 new units of one device copy units of one old device, and some pair of devices reaches 40.
All inputs are finite; a program needn't handle non-finite values.
Results may differ from a plain program's by a relative error of at most 0.0049.
Values may be sent and summed in bfloat16 or wider, within the bound.
No kernel may reach another device: no remote copies, remote signals or barrier semaphores. Data moves between devices by JAX's collectives and lax.ppermute only.
A program may use at most 64 MiB of HBM per device.

v0:
```python
import jax
import jax.numpy as jnp
from jax import lax
from jax.sharding import PartitionSpec as P

D_OLD = 6144
D_NEW = 8192


def owners(bounds, unit_ids):
    return jnp.sum((bounds[None, 1:] <= unit_ids[:, None]).astype(jnp.int32), axis=1)


def routing(
    owner_of,
    local_of,
    table_rows,
    slot_cap,
    dev_index,
    dest_owner,
    new_bounds,
    positions,
    wanted,
    own_slots,
    dp_count,
):
    from_me = (owner_of == dev_index).astype(jnp.int32)
    before = jnp.cumsum(from_me) - from_me
    send_slot = before - before[new_bounds[dest_owner]]
    target = jnp.where(from_me > 0, dest_owner * slot_cap + send_slot, dp_count * slot_cap)
    chosen = jnp.zeros((dp_count * slot_cap,), jnp.int32).at[target].set(positions, mode="drop")
    filled = jnp.zeros((dp_count * slot_cap,), jnp.bool_).at[target].set(True, mode="drop")
    local_row = jnp.clip(local_of[chosen], 0, table_rows - 1)
    anchor = owner_of[wanted]
    earlier = (own_slots[None, :] < own_slots[:, None]) & (anchor[None, :] == anchor[:, None])
    arrival_rank = jnp.sum(earlier.astype(jnp.int32), axis=1)
    incoming = jnp.minimum(anchor * slot_cap + arrival_rank, dp_count * slot_cap - 1)
    return (local_row, filled, incoming)


def outgoing(source_table, route_info):
    return jnp.where(
        route_info[1][:, None], source_table[route_info[0]], jnp.zeros((), source_table.dtype)
    )


def arrived(source_table, route_info, live_new):
    return jnp.where(live_new[:, None], source_table[route_info[2]], 0.0)


def on_device(
    hidden_old,
    cotangent,
    gain_old,
    old_bounds,
    new_bounds,
    source_map,
    weight_old,
    moment_first,
    moment_second,
):
    dp_count = lax.axis_size("dp")
    dev_index = lax.axis_index("dp")
    old_cap = weight_old.shape[0]
    new_mean = D_NEW // dp_count
    new_cap = new_mean + new_mean // 4
    pair_cap = (new_cap + dp_count - 1) // dp_count
    positions = jnp.arange(D_NEW, dtype=jnp.int32)
    first_use = jnp.full((D_OLD,), D_NEW, jnp.int32).at[source_map].min(positions)
    unit_used = first_use < D_NEW
    keep_mask = first_use[source_map] == positions
    copies = jnp.zeros((D_OLD,), jnp.float32).at[source_map].add(1.0)
    padded = jnp.arange(dp_count * old_cap, dtype=jnp.int32)
    slot_owner = padded // old_cap
    within = padded - slot_owner * old_cap
    live_old = within < old_bounds[slot_owner + 1] - old_bounds[slot_owner]
    slot_unit = jnp.minimum(old_bounds[slot_owner] + within, D_OLD - 1)
    weight_live = live_old & unit_used[slot_unit]
    source_owner = owners(old_bounds, source_map)
    source_slot = source_owner * old_cap + source_map - old_bounds[source_owner]
    dest_owner = owners(new_bounds, positions)
    own_slots = jnp.arange(new_cap, dtype=jnp.int32)
    live_new = own_slots < new_bounds[dev_index + 1] - new_bounds[dev_index]
    wanted = jnp.minimum(new_bounds[dev_index] + own_slots, D_NEW - 1)
    grad_route = routing(
        source_owner,
        source_map - old_bounds[dev_index],
        old_cap,
        pair_cap,
        dev_index,
        dest_owner,
        new_bounds,
        positions,
        wanted,
        own_slots,
        dp_count,
    )
    moment_route = routing(
        source_owner,
        source_map - old_bounds[dev_index],
        old_cap,
        pair_cap,
        dev_index,
        dest_owner,
        new_bounds,
        positions,
        wanted,
        own_slots,
        dp_count,
    )
    stream = hidden_old.astype(jnp.float32)
    squares = jnp.sum(stream * stream * copies, axis=1)
    inv_rms = lax.rsqrt(squares / D_NEW + 1e-05)
    normed = (stream * inv_rms[:, None] * gain_old).astype(jnp.bfloat16)
    normed_slots = jnp.take(normed, slot_unit, axis=1)
    hidden_slots = jnp.take(hidden_old, slot_unit, axis=1)
    weight_block = lax.all_gather(weight_old, "dp", axis=0, tiled=True)
    masked_block = jnp.where(weight_live[:, None], weight_block, jnp.zeros((), weight_block.dtype))
    columns = normed_slots
    key_sums = jnp.dot(columns, masked_block, preferred_element_type=jnp.float32)
    slopes = lax.dot_general(
        cotangent, masked_block, (((1,), (1,)), ((), ())), preferred_element_type=jnp.float32
    )
    scaled = hidden_slots.astype(jnp.float32) * inv_rms[:, None]
    column_terms = jnp.sum(slopes * scaled, axis=0)
    key_sums, column_terms = (key_sums, column_terms)
    projected = key_sums.astype(jnp.bfloat16)
    columns = normed_slots
    grad_own = lax.psum_scatter(
        lax.dot_general(
            columns, cotangent, (((0,), (0,)), ((), ())), preferred_element_type=jnp.float32
        ),
        "dp",
        scatter_dimension=0,
        tiled=True,
    )
    grad_own = lax.psum(grad_own.astype(jnp.bfloat16), "rep").astype(jnp.float32)
    column_total = lax.psum(column_terms, ("dp", "rep"))
    gain_grad = jnp.where(keep_mask, column_total[source_slot], 0.0)
    moved_grad, moved_first, moved_second = (
        lax.all_to_all(
            outgoing(grad_own, grad_route), "dp", split_axis=0, concat_axis=0, tiled=True
        ),
        lax.all_to_all(
            outgoing(moment_first, moment_route), "dp", split_axis=0, concat_axis=0, tiled=True
        ),
        lax.all_to_all(
            outgoing(moment_second, moment_route), "dp", split_axis=0, concat_axis=0, tiled=True
        ),
    )
    grad_new = arrived(moved_grad, grad_route, live_new)
    first_next = jnp.where(
        live_new[:, None], 0.9 * arrived(moved_first, moment_route, live_new) + 0.1 * grad_new, 0.0
    )
    second_next = jnp.where(
        live_new[:, None],
        0.95 * arrived(moved_second, moment_route, live_new) + 0.05 * grad_new * grad_new,
        0.0,
    )
    adam_step = first_next / (jnp.sqrt(second_next) + 1e-08)
    return (projected, gain_grad, first_next, second_next, adam_step)


def solution(mesh):
    placed = (
        P(("dp", "rep"), None),
        P(("dp", "rep"), None),
        P(),
        P(),
        P(),
        P(),
        P("dp", None),
        P("dp", None),
        P("dp", None),
    )
    return jax.shard_map(
        on_device,
        mesh=mesh,
        in_specs=placed,
        out_specs=(P(("dp", "rep"), None), P(), P("dp", None), P("dp", None), P("dp", None)),
        check_vma=False,
    )
```

profile of v0, /device:TPU:0, one launch (start us, length us, event | category | flops | bytes accessed | tf_op | source)
XLA Modules:
  0.0 749.6 jit_solution(12491640202311818620)
XLA Ops:
  7.8 2.0 fusion.43
  9.9 4.5 compare_select_fusion.25
  14.4 6.3 compare_and_fusion
  20.7 3.2 copy.20
  23.9 1.3 broadcast_subtract_fusion
  25.8 44.6 %scatter_custom_fusion = f32[6144]{0:T(1024)} fusion(s32[8192]{0:T(1024)} %get-tuple-element.42, f32[8192]{0:T(1024)} %broadcast.609, f32[]{:T(128)} %constant.37.clone.1), kind=kCustom, calls=%fused_computation.165 | custom fusion | flops 8192 | bytes 25088 | tf_op jit(solution)/shard_map/scatter-add | solution.py:72
  70.5 1.7 fusion.2
  72.2 2.9 fusion.4
  75.0 33.2 %gather_fusion.12 = bf16[8192,256]{1,0:T(8,128)(2,1)} fusion(bf16[256,6144]{0,1:T(8,128)(2,1)} %fusion.4, s32[8192]{0:T(1024)S(1)} %broadcast_clamp_fusion.3), kind=kCustom, calls=%fused_computation.clone | custom fusion | bytes 8421376 | tf_op jit(solution)/shard_map/jit(_take)/gather | solution.py:115
  108.2 7.2 fusion.5
  115.5 98.0 %reduce-scatter.2.cloned.1.call-done = f32[512,128]{1,0:T(8,128)} async-done(((f32[8192,128]{1,0:T(8,128)}), f32[512,128]{1,0:T(8,128)}) %reduce-scatter.2.cloned.1.call-update) | async-done | bytes 262160 | tf_op jit(solution)/shard_map/reduce_scatter | solution.py:129
  213.5 1.6 convert_element_type.58
  215.1 0.7 all-gather.2.cloned.1.call-update
  217.1 0.7 fusion.42
  218.0 4.5 compare_select_fusion.7
  222.6 1.0 compare_reduce_fusion.9
  223.5 6.2 select_select_fusion
  230.5 0.8 convert_reduce_fusion.2
  231.9 1.0 reduce-window.9
  233.0 0.7 slice.117
  233.7 1.4 reduce-window.12
  235.1 0.9 slice_reduce_fusion
  236.0 1.5 convert_subtract_fusion
  237.4 80.7 %gather_fusion.3 = s32[8192]{0:T(1024)} fusion(s32[8192]{0:T(1024)S(1)} %get-tuple-element.31, s32[8192]{0:T(1024)} %broadcast_clamp_fusion), kind=kCustom, calls=%fused_computation.5 | custom fusion | bytes 98304 | tf_op jit(solution)/shard_map/gather | solution.py:29
  318.1 6.1 compare_select_fusion.13
  324.2 30.8 %scatter_custom_fusion.3 = s32[640]{0:T(1024)S(1)} fusion(s32[8192]{0:T(1024)} %bitcast.97, s32[8192]{0:T(1024)S(1)} %iota.49, s32[]{:T(128)} %constant.38.clone.1), kind=kCustom, calls=%fused_computation.178 | custom fusion | bytes 3072 | tf_op jit(solution)/shard_map/scatter | solution.py:31
  355.1 3.9 gather_fusion.4
  359.0 2.3 gather_fusion.5
  361.2 3.2 gather_fusion.10
  364.5 34.7 %scatter_custom_fusion.2 = pred[640]{0:T(1024)(128)(4,1)S(1)} fusion(s32[8192]{0:T(1024)} %bitcast.98, pred[8192]{0:T(1024)(128)(4,1)S(1)} %broadcast.610, pred[]{:T(512)} %constant.95.clone.1), kind=kCustom, calls=%fused_computation.180 | custom fusion | bytes 1152 | tf_op jit(solution)/shard_map/scatter | solution.py:32
  399.2 0.7 broadcast_in_dim.153
  399.9 0.7 fusion.31
  400.6 3.9 gather_fusion.6
  406.4 44.3 %scatter_custom_fusion.1 = s32[6144]{0:T(1024)S(1)} fusion(s32[8192]{0:T(1024)} %get-tuple-element.42, s32[8192]{0:T(1024)} %iota.45, s32[]{:T(128)} %constant.34.clone.1), kind=kCustom, calls=%fused_computation.163 | custom fusion | flops 8192 | bytes 25088 | tf_op jit(solution)/shard_map/scatter-min | solution.py:69
  451.0 0.7 compare_reduce_fusion.20
  451.7 0.6 compare_reduce_fusion.21
  452.3 0.6 compare_reduce_fusion.22
  453.0 0.6 compare_reduce_fusion.23
  453.6 0.6 compare_reduce_fusion.24
  454.3 0.6 compare_reduce_fusion.25
  454.9 0.6 compare_reduce_fusion.26
  456.2 0.6 compare_reduce_fusion.28
  458.2 1.6 convert_element_type.59
  459.8 3.2 gather_fusion.8
  463.0 2.3 broadcast_select_fusion.8
  465.2 5.2 all-to-all-start.2
  470.5 0.6 compare_reduce_fusion.29
  471.1 32.9 %gather_fusion.13 = bf16[8192,256]{1,0:T(8,128)(2,1)} fusion(bf16[256,6144]{0,1:T(8,128)(2,1)S(1)} %copy.20, s32[8192]{0:T(1024)S(1)} %copy-done.6), kind=kCustom, calls=%fused_computation.1.clone | custom fusion | bytes 8421376 | tf_op jit(solution)/shard_map/jit(_take)/gather | solution.py:116
  504.1 6.4 copy.22
  510.5 45.5 %gather_fusion.1 = s32[8192]{0:T(1024)S(1)} fusion(s32[6144]{0:T(1024)S(1)} %scatter_custom_fusion.1, s32[8192]{0:T(1024)S(1)} %copy-done.13), kind=kCustom, calls=%fused_computation.3 | custom fusion | bytes 98304 | tf_op jit(solution)/shard_map/gather | solution.py:71
  556.2 50.7 %gather_fusion = pred[8192]{0:T(1024)(128)(4,1)S(1)} fusion(pred[6144]{0:T(1024)(128)(4,1)S(1)} %broadcast_compare_fusion.1, s32[8192]{0:T(1024)S(1)} %copy-done.9), kind=kCustom, calls=%fused_computation.2 | custom fusion | bytes 49152 | tf_op jit(solution)/shard_map/gather | solution.py:78
  606.9 1.0 compare_reduce_fusion.19
  608.0 6.3 fusion.25
  614.3 6.3 fusion.22
  620.7 6.9 all-to-all-start
  627.6 7.3 fusion.9
  635.0 40.8 %psum.14 = f32[8192]{0:T(1024)S(1)} all-reduce(f32[8192]{0:T(1024)S(1)} %fusion.9), channel_id=1, replica_groups=mesh['dp'=16,'rep'=2] {'dp','rep'}, use_global_device_ids=true, to_apply=%region_4.6 | all-reduce | flops 8192 | bytes 65536 | tf_op jit(solution)/shard_map/psum | solution.py:138
  675.8 45.5 %gather_fusion.2 = f32[8192]{0:T(1024)S(1)} fusion(f32[8192]{0:T(1024)S(1)} %psum.14, s32[8192]{0:T(1024)S(1)} %fusion.22), kind=kCustom, calls=%fused_computation.4 | custom fusion | bytes 98304 | tf_op jit(solution)/shard_map/gather | solution.py:139
  721.4 5.4 all-to-all-start.1
  727.4 8.4 %fusion.11 = bf16[256,128]{1,0:T(8,128)(2,1)} fusion(bf16[8192,256]{1,0:T(8,128)(2,1)} %gather_fusion.12, pred[8192]{0:T(1024)(128)(4,1)S(1)} %get-tuple-element.37, bf16[8192,128]{1,0:T(8,128)(2,1)S(1)} %copy-done.28, pred[8192]{0:T(1024)(128)(4,1)S(1)} %fusion.25), kind=kOutput, calls=%fused_computation.36 | convolution fusion | flops 540049408 | bytes 6373376 | tf_op jit(solution)/shard_map/dot_general | solution.py:120
  735.8 2.6 gather_fusion.11
  738.4 1.7 gather_fusion.7
  740.1 1.7 gather_fusion.9
  741.8 1.2 add_divide_fusion
  (107 shorter events, 7.8 us)
Async XLA Ops:
  7.2 351.8 %copy-start = (f32[512,128]{1,0:T(8,128)S(1)}, f32[512,128]{1,0:T(8,128)}, u32[]{:S(2)}) copy-start(f32[512,128]{1,0:T(8,128)} %param.18) | copy-start | bytes 786436
  7.2 16.8 %copy-start.2 = (s32[8192]{0:T(1024)S(1)}, s32[8192]{0:T(1024)}, u32[]{:S(2)}) copy-start(s32[8192]{0:T(1024)} %param.16) | copy-start | bytes 98308
  7.2 206.3 %reduce-scatter.2.cloned.1.call-start = ((), (), s32[]{:S(2)}) async-start(), calls=%async_computation.5 | async-start | bytes 4456448 | tf_op jit(solution)/shard_map/reduce_scatter | solution.py:129
  20.7 54.3 %copy-start.5 = (s32[8192]{0:T(1024)}, s32[8192]{0:T(1024)S(1)}, u32[]{:S(2)}) copy-start(s32[8192]{0:T(1024)S(1)} %broadcast_clamp_fusion.3) | copy-start | bytes 98308
  72.2 36.1 %copy-start.25 = (f32[256]{0:T(256)}, f32[256]{0:T(256)S(1)}, u32[]{:S(2)}) copy-start(f32[256]{0:T(256)S(1)} %add_rsqrt_fusion) | copy-start | bytes 3076
  115.4 100.4 %copy-start.8 = (s32[17]{0:T(128)S(1)}, s32[17]{0:T(128)}, u32[]{:S(2)}) copy-start(s32[17]{0:T(128)} %param.15) | copy-start | bytes 208
  115.4 101.1 %copy-start.7 = (s32[17]{0:T(128)S(1)}, s32[17]{0:T(128)}, u32[]{:S(2)}) copy-start(s32[17]{0:T(128)} %param.14) | copy-start | bytes 208
  115.4 342.7 %all-reduce.2.cloned.1.call-start = ((), (), s32[]{:S(2)}) async-start(), calls=%async_computation.6 | async-start | bytes 262144 | tf_op jit(solution)/shard_map/psum | solution.py:137
  215.1 412.5 %all-gather.2.cloned.1.call-start = ((), (), s32[]{:S(2)}) async-start(), calls=%async_computation.4 | async-start | bytes 2228224 | tf_op jit(solution)/shard_map/all_gather | solution.py:117
  218.0 11.8 %copy-start.4 = (s32[8192]{0:T(1024)}, s32[8192]{0:T(1024)S(1)}, u32[]{:S(2)}) copy-start(s32[8192]{0:T(1024)S(1)} %convert_reduce_fusion.1) | copy-start | bytes 98308
  233.0 3.0 copy-start.1
  404.4 66.7 %copy-start.6 = (s32[8192]{0:T(1024)S(1)}, s32[8192]{0:T(1024)}, u32[]{:S(2)}) copy-start(s32[8192]{0:T(1024)} %copy-done.5) | copy-start | bytes 98308
  465.2 155.4 %all-to-all-start.2 = ((f32[16,40,128]{2,1,0:T(8,128)}), f32[16,40,128]{2,1,0:T(8,128)}, u32[]{:S(2)}, u32[]{:S(2)}) async-start(f32[16,40,128]{2,1,0:T(8,128)} %get-tuple-element.45), calls=%async_computation.3 | async-start | bytes 655360 | tf_op jit(solution)/shard_map/all_to_all | solution.py:147
  504.1 6.4 copy-start.13
  510.4 45.5 %copy-start.9 = (s32[8192]{0:T(1024)S(1)}, s32[8192]{0:T(1024)}, u32[]{:S(2)}) copy-start(s32[8192]{0:T(1024)} %broadcast_clamp_fusion.2) | copy-start | bytes 98308
  556.0 50.9 %copy-start.10 = (s32[8192,1]{0,1:T(1,128)S(1)}, s32[8192,1]{0,1:T(1,128)}, u32[]{:S(2)}) copy-start(s32[8192,1]{0,1:T(1,128)} %get-tuple-element.36) | copy-start | bytes 98308
  556.0 51.9 %copy-start.12 = (s32[8192,1]{0,1:T(1,128)S(1)}, s32[8192,1]{0,1:T(1,128)}, u32[]{:S(2)}) copy-start(s32[8192,1]{0,1:T(1,128)} %get-tuple-element.82) | copy-start | bytes 98308
  556.0 51.9 %copy-start.15 = (pred[8192]{0:T(1024)(128)(4,1)S(1)}, pred[8192]{0:T(1024)(128)(4,1)}, u32[]{:S(2)}) copy-start(pred[8192]{0:T(1024)(128)(4,1)} %compare_reduce_fusion.20) | copy-start | bytes 24580
  556.0 51.9 %copy-start.16 = (pred[8192]{0:T(1024)(128)(4,1)S(1)}, pred[8192]{0:T(1024)(128)(4,1)}, u32[]{:S(2)}) copy-start(pred[8192]{0:T(1024)(128)(4,1)} %compare_reduce_fusion.21) | copy-start | bytes 24580
  556.0 51.9 %copy-start.17 = (pred[8192]{0:T(1024)(128)(4,1)S(1)}, pred[8192]{0:T(1024)(128)(4,1)}, u32[]{:S(2)}) copy-start(pred[8192]{0:T(1024)(128)(4,1)} %compare_reduce_fusion.22) | copy-start | bytes 24580
  556.0 51.9 %copy-start.18 = (pred[8192]{0:T(1024)(128)(4,1)S(1)}, pred[8192]{0:T(1024)(128)(4,1)}, u32[]{:S(2)}) copy-start(pred[8192]{0:T(1024)(128)(4,1)} %compare_reduce_fusion.23) | copy-start | bytes 24580
  556.1 51.9 %copy-start.19 = (pred[8192]{0:T(1024)(128)(4,1)S(1)}, pred[8192]{0:T(1024)(128)(4,1)}, u32[]{:S(2)}) copy-start(pred[8192]{0:T(1024)(128)(4,1)} %compare_reduce_fusion.24) | copy-start | bytes 24580
  556.1 51.9 %copy-start.20 = (pred[8192]{0:T(1024)(128)(4,1)S(1)}, pred[8192]{0:T(1024)(128)(4,1)}, u32[]{:S(2)}) copy-start(pred[8192]{0:T(1024)(128)(4,1)} %compare_reduce_fusion.25) | copy-start | bytes 24580
  556.1 51.9 %copy-start.21 = (pred[8192]{0:T(1024)(128)(4,1)S(1)}, pred[8192]{0:T(1024)(128)(4,1)}, u32[]{:S(2)}) copy-start(pred[8192]{0:T(1024)(128)(4,1)} %compare_reduce_fusion.26) | copy-start | bytes 24580
  556.1 51.9 %copy-start.22 = (pred[8192]{0:T(1024)(128)(4,1)S(1)}, pred[8192]{0:T(1024)(128)(4,1)}, u32[]{:S(2)}) copy-start(pred[8192]{0:T(1024)(128)(4,1)} %compare_reduce_fusion.27) | copy-start | bytes 24580
  556.1 51.9 %copy-start.23 = (pred[8192]{0:T(1024)(128)(4,1)S(1)}, pred[8192]{0:T(1024)(128)(4,1)}, u32[]{:S(2)}) copy-start(pred[8192]{0:T(1024)(128)(4,1)} %compare_reduce_fusion.28) | copy-start | bytes 24580
  556.1 51.9 %copy-start.24 = (pred[8192]{0:T(1024)(128)(4,1)S(1)}, pred[8192]{0:T(1024)(128)(4,1)}, u32[]{:S(2)}) copy-start(pred[8192]{0:T(1024)(128)(4,1)} %compare_reduce_fusion.29) | copy-start | bytes 24580
  556.1 58.2 %copy-start.3 = (s32[8192]{0:T(1024)S(1)}, s32[8192]{0:T(1024)}, u32[]{:S(2)}) copy-start(s32[8192]{0:T(1024)} %param.16) | copy-start | bytes 98308
  556.1 58.2 %copy-start.11 = (s32[8192,1]{0,1:T(1,128)S(1)}, s32[8192,1]{0,1:T(1,128)}, u32[]{:S(2)}) copy-start(s32[8192,1]{0,1:T(1,128)} %get-tuple-element.35) | copy-start | bytes 98308
  556.1 71.5 %copy-start.14 = (bf16[256,128]{1,0:T(8,128)(2,1)S(1)}, bf16[256,128]{1,0:T(8,128)(2,1)}, u32[]{:S(2)}) copy-start(bf16[256,128]{1,0:T(8,128)(2,1)} %param.12) | copy-start | bytes 196612
  556.1 71.5 %copy-start.26 = (f32[256]{0:T(256)S(1)}, f32[256]{0:T(256)}, u32[]{:S(2)}) copy-start(f32[256]{0:T(256)} %copy-done.25) | copy-start | bytes 3076
  620.7 100.7 %all-to-all-start = ((f32[16,40,128]{2,1,0:T(8,128)}), f32[16,40,128]{2,1,0:T(8,128)S(1)}, u32[]{:S(2)}, u32[]{:S(2)}) async-start(f32[16,40,128]{2,1,0:T(8,128)} %get-tuple-element.43), calls=%async_computation | async-start | bytes 655360 | tf_op jit(solution)/shard_map/all_to_all | solution.py:144
  675.8 51.6 %copy-start.28 = (bf16[8192,128]{1,0:T(8,128)(2,1)S(1)}, bf16[8192,128]{1,0:T(8,128)(2,1)}, u32[]{:S(2)}) copy-start(bf16[8192,128]{1,0:T(8,128)(2,1)} %all-gather.2.cloned.1.call-done) | copy-start | bytes 6291460
  721.4 18.7 %all-to-all-start.1 = ((f32[16,40,128]{2,1,0:T(8,128)}), f32[16,40,128]{2,1,0:T(8,128)S(1)}, u32[]{:S(2)}, u32[]{:S(2)}) async-start(f32[16,40,128]{2,1,0:T(8,128)} %get-tuple-element.44), calls=%async_computation.2 | async-start | bytes 655360 | tf_op jit(solution)/shard_map/all_to_all | solution.py:141
  735.8 6.0 copy-start.27
Sparse Core Ops, SparseCore 0:
  115.6 97.8 reduce-scatter.1
  216.3 17.4 all-reduce.1
  236.6 61.8 all-gather.1
where the time goes:
time: 752 us; the launch traced here: 750 us
  local copies, waits for them, and re-layouts  394 us (52%)
  other arithmetic  160 us (21%)
  waiting for transfers between devices  98.7 us (13%)
  blocking collectives  40.8 us (5%)
  matrix products  22.9 us (3%)
  starting transfers between devices  17.7 us (2%)
  between operations  15.8 us (2%)
    reduce_scatter x1, waiting for transfers between devices, on_device(): lax.psum_scatter(lax.dot_general(columns, cotangent, (((0,), (0,)), ((),...  98 us
    gather x2, local copies, waits for them, and re-layouts, routing(): send_slot = before - before[new_bounds[dest_owner]]  81.3 us
    gather x1, local copies, waits for them, and re-layouts, on_device(): weight_live = live_old & unit_used[slot_unit]  50.7 us
    gather x1, local copies, waits for them, and re-layouts, on_device(): gain_grad = jnp.where(keep_mask, column_total[source_slot], 0.0)  45.5 us
    gather x1, local copies, waits for them, and re-layouts, on_device(): keep_mask = first_use[source_map] == positions  45.5 us
    scatter-add x1, other arithmetic, on_device(): copies = jnp.zeros((D_OLD,), jnp.float32).at[source_map].add(1.0)  44.6 us
    another operation x1, other arithmetic, on_device(): jnp.full((D_OLD,), D_NEW, jnp.int32).at[source_map].min(positions)  44.3 us
    psum x1, blocking collectives, on_device(): column_total = lax.psum(column_terms, ('dp', 'rep'))  40.8 us
  transfers between devices with their start and end apart: 6, of which 1 were waited for; matrix products, arithmetic and copies ran while one was open for 62% of the time, Pallas kernels for 0%

commit v1 on v0

--- a/solution.py
+++ b/solution.py
@@ -135,7 +135,7 @@
         tiled=True,
     )
     grad_own = lax.psum(grad_own.astype(jnp.bfloat16), "rep").astype(jnp.float32)
-    column_total = lax.psum(column_terms, ("dp", "rep"))
+    column_total = jnp.sum(lax.all_gather(column_terms, ("dp", "rep")), axis=0)
     gain_grad = jnp.where(keep_mask, column_total[source_slot], 0.0)
     moved_grad, moved_first, moved_second = (
         lax.all_to_all(

time: 752 us -> 625 us (0.83)
  waiting for transfers between devices: 98.7 us -> 20.9 us
  blocking collectives: 40.8 us -> 0 us
  other arithmetic: 160 us -> 150 us
    reduce_scatter x1, waiting for transfers between devices: 98 us -> 0.02 us  [on_device(): lax.psum_scatter(lax.dot_general(columns, cotangent, (((0,), (0,)), ((),...]
    psum x1 -> x0, blocking collectives: 40.8 us -> none  [on_device(): column_total = lax.psum(column_terms, ('dp', 'rep'))]
    psum x1, waiting for transfers between devices: 0.01 us -> 12.7 us  [on_device(): lax.psum(grad_own.astype(jnp.bfloat16), 'rep').astype(jnp.float32)]
  transfers between devices with their start and end apart: 6 -> 7, of which waited for: 1 -> 2; matrix products, arithmetic and copies ran while one was open for 62% -> 73% of each run, Pallas kernels for 0% -> 0%
where the time goes in v1:
time: 625 us; the launch traced here: 622 us
  local copies, waits for them, and re-layouts  392 us (63%)
  other arithmetic  150 us (24%)
  matrix products  25.4 us (4%)
  waiting for transfers between devices  20.9 us (3%)
  starting transfers between devices  17.4 us (3%)
  between operations  15.6 us (2%)
    gather x2, local copies, waits for them, and re-layouts, routing(): send_slot = before - before[new_bounds[dest_owner]]  81.2 us
    gather x1, local copies, waits for them, and re-layouts, on_device(): weight_live = live_old & unit_used[slot_unit]  50.7 us
    gather x1, local copies, waits for them, and re-layouts, on_device(): keep_mask = first_use[source_map] == positions  45.5 us
    gather x1, local copies, waits for them, and re-layouts, on_device(): gain_grad = jnp.where(keep_mask, column_total[source_slot], 0.0)  45.5 us
    scatter-add x1, other arithmetic, on_device(): copies = jnp.zeros((D_OLD,), jnp.float32).at[source_map].add(1.0)  44.6 us
    another operation x1, other arithmetic, on_device(): jnp.full((D_OLD,), D_NEW, jnp.int32).at[source_map].min(positions)  44.4 us
    gather x2, local copies, waits for them, and re-layouts, on_device(): hidden_slots = jnp.take(hidden_old, slot_unit, axis=1)  41.9 us
    scatter x1, local copies, waits for them, and re-layouts, routing(): jnp.zeros((dp_count * slot_cap,), jnp.bool_).at[target]  34.7 us
  transfers between devices with their start and end apart: 7, of which 2 were waited for; matrix products, arithmetic and copies ran while one was open for 73% of the time, Pallas kernels for 0%

profile of v1, /device:TPU:0, one launch (start us, length us, event | category | flops | bytes accessed | tf_op | source)
XLA Modules:
  0.0 622.0 jit_solution(15385956993078225056)
XLA Ops:
  7.8 2.0 fusion.43
  9.8 4.4 compare_select_fusion.25
  14.3 6.3 %compare_and_fusion = (pred[8192]{0:T(1024)(128)(4,1)S(1)}, s32[8192]{0:T(1024)S(1)}) fusion(pred[8192]{0:T(1024)(128)(4,1)S(1)} %compare_reduce_fusion.30, pred[8192]{0:T(1024)(128)(4,1)S(1)} %compare_reduce_fusion.31, pred[8192]{0:T(1024)(128)(4,1)S(1)} %compare_reduce_fusion.32, pred[8192]{0:T(1024)(128)(4,1)S(1)} %compare_reduce_fusion.33, ...), kind=kLoop, calls=%fused_computation.150 | loop fusion | flops 229376 | bytes 155688 | tf_op jit(solution)/shard_map/jit(_take)/and | solution.py:115
  20.6 3.2 copy.23
  23.8 1.3 broadcast_subtract_fusion
  25.1 0.6 broadcast.609
  25.7 44.6 %scatter_custom_fusion = f32[6144]{0:T(1024)} fusion(s32[8192]{0:T(1024)} %get-tuple-element.42, f32[8192]{0:T(1024)} %broadcast.609, f32[]{:T(128)} %constant.37.clone.1), kind=kCustom, calls=%fused_computation.165 | custom fusion | flops 8192 | bytes 25088 | tf_op jit(solution)/shard_map/scatter-add | solution.py:72
  70.4 1.7 fusion.2
  72.1 0.6 copy-done.13
  72.6 2.9 fusion.4
  75.5 33.2 %gather_fusion.12 = bf16[8192,256]{1,0:T(8,128)(2,1)} fusion(bf16[256,6144]{0,1:T(8,128)(2,1)} %fusion.4, s32[8192]{0:T(1024)S(1)} %broadcast_clamp_fusion.3), kind=kCustom, calls=%fused_computation.clone | custom fusion | bytes 8421376 | tf_op jit(solution)/shard_map/jit(_take)/gather | solution.py:115
  108.7 7.2 %fusion.5 = f32[8192,128]{1,0:T(8,128)} fusion(bf16[256,128]{1,0:T(8,128)(2,1)} %param.12, bf16[8192,256]{1,0:T(8,128)(2,1)} %gather_fusion.12, pred[8192]{0:T(1024)(128)(4,1)S(1)} %get-tuple-element.37), kind=kOutput, calls=%fused_computation.26 | convolution fusion | flops 538968064 | bytes 8462336 | tf_op jit(solution)/shard_map/dot_general | solution.py:130
  116.0 0.7 all-gather.4.cloned.1.call-update
  116.8 0.5 slice.88
  117.4 0.7 fusion.42
  118.1 0.2 convert_reduce_fusion.1
  118.3 0.6 copy-done.5
  118.9 4.4 compare_select_fusion.7
  123.3 1.0 compare_reduce_fusion.9
  124.3 6.2 %select_select_fusion = s32[8192]{0:T(1024)S(1)} fusion(pred[8192]{0:T(1024)(128)(4,1)S(1)} %get-tuple-element.15, pred[8192]{0:T(1024)(128)(4,1)S(1)} %get-tuple-element.14, pred[8192]{0:T(1024)(128)(4,1)S(1)} %get-tuple-element.13, pred[8192]{0:T(1024)(128)(4,1)S(1)} %get-tuple-element.12, pred[8192]{0:T(1024)(128)(4,1)S(1)} %get-tuple-element.11, ...), kind=kLoop, calls=%fused_computation.143 | loop fusion | flops 81920 | bytes 147496 | tf_op jit(solution)/shard_map/gather | solution.py:29
  130.6 0.6 broadcast_clamp_fusion
  131.2 0.2 convert_reduce_fusion.2
  131.4 0.6 convert_bitcast_fusion
  132.0 1.0 reduce-window.9
  133.1 0.7 slice.117
  133.8 1.4 reduce-window.12
  135.2 0.9 slice_reduce_fusion
  136.1 1.5 convert_subtract_fusion
  137.5 80.7 %gather_fusion.3 = s32[8192]{0:T(1024)} fusion(s32[8192]{0:T(1024)S(1)} %get-tuple-element.31, s32[8192]{0:T(1024)} %broadcast_clamp_fusion), kind=kCustom, calls=%fused_computation.5 | custom fusion | bytes 98304 | tf_op jit(solution)/shard_map/gather | solution.py:29
  218.2 6.1 compare_select_fusion.13
  224.3 35.6 %gather_fusion.13 = bf16[8192,256]{1,0:T(8,128)(2,1)} fusion(bf16[256,6144]{0,1:T(8,128)(2,1)S(1)} %copy.23, s32[8192]{0:T(1024)} %copy-done.6), kind=kCustom, calls=%fused_computation.1.clone | custom fusion | bytes 8421376 | tf_op jit(solution)/shard_map/jit(_take)/gather | solution.py:116
  259.9 30.9 %scatter_custom_fusion.3 = s32[640]{0:T(1024)S(1)} fusion(s32[8192]{0:T(1024)} %bitcast.98, s32[8192]{0:T(1024)S(1)} %iota.49, s32[]{:T(128)} %constant.38.clone.1), kind=kCustom, calls=%fused_computation.178 | custom fusion | bytes 3072 | tf_op jit(solution)/shard_map/scatter | solution.py:31
  290.8 3.9 gather_fusion.4
  294.8 1.7 gather_fusion.5
  296.4 1.7 gather_fusion.10
  298.1 34.7 %scatter_custom_fusion.2 = pred[640]{0:T(1024)(128)(4,1)S(1)} fusion(s32[8192]{0:T(1024)} %bitcast.99, pred[8192]{0:T(1024)(128)(4,1)S(1)} %broadcast.610, pred[]{:T(512)} %constant.95.clone.1), kind=kCustom, calls=%fused_computation.180 | custom fusion | bytes 1152 | tf_op jit(solution)/shard_map/scatter | solution.py:32
  332.9 6.4 %copy.25 = bf16[8192,256]{0,1:T(8,128)(2,1)} copy(bf16[8192,256]{1,0:T(8,128)(2,1)} %gather_fusion.13) | data formatting | bytes 8388608 | tf_op jit(solution)/shard_map/jit(_take)/gather | solution.py:116
  339.3 44.4 %scatter_custom_fusion.1 = s32[6144]{0:T(1024)S(1)} fusion(s32[8192]{0:T(1024)} %get-tuple-element.42, s32[8192]{0:T(1024)S(1)} %iota.45, s32[]{:T(128)} %constant.34.clone.1), kind=kCustom, calls=%fused_computation.163 | custom fusion | flops 8192 | bytes 25088 | tf_op jit(solution)/shard_map/scatter-min | solution.py:69
  383.8 50.7 %gather_fusion = pred[8192]{0:T(1024)(128)(4,1)S(1)} fusion(pred[6144]{0:T(1024)(128)(4,1)S(1)} %broadcast_compare_fusion.1, s32[8192]{0:T(1024)S(1)} %broadcast_clamp_fusion.2), kind=kCustom, calls=%fused_computation.2 | custom fusion | bytes 49152 | tf_op jit(solution)/shard_map/gather | solution.py:78
  435.1 6.3 %fusion.25 = pred[8192]{0:T(1024)(128)(4,1)S(1)} fusion(pred[8192]{0:T(1024)(128)(4,1)S(1)} %gather_fusion, s32[8192]{0:T(1024)S(1)} %get-tuple-element.38, pred[8192]{0:T(1024)(128)(4,1)S(1)} %compare_reduce_fusion.20, pred[8192]{0:T(1024)(128)(4,1)S(1)} %compare_reduce_fusion.21, pred[8192]{0:T(1024)(128)(4,1)S(1)} %compare_reduce_fusion.22, ...), kind=kLoop, calls=%fused_computation.151 | loop fusion | flops 188416 | bytes 163880 | tf_op jit(solution)/shard_map/and | solution.py:78
  441.5 1.6 convert_element_type.58
  443.2 7.9 %fusion.9 = f32[8192]{0:T(1024)} fusion(f32[256]{0:T(256)S(1)} %copy-done.14, bf16[8192,256]{0,1:T(8,128)(2,1)} %copy.25, pred[8192]{0:T(1024)(128)(4,1)S(1)} %get-tuple-element.37, bf16[256,128]{1,0:T(8,128)(2,1)S(1)} %copy-done.12, bf16[8192,128]{1,0:T(8,128)(2,1)} %all-gather.4.cloned.1.call-done, pred[8192]{0:T(1024)(128)(4,1)S(1)} %fusion.25), kind=kOutput, calls=%fused_computation.31 | convolution fusion | flops 548397056 | bytes 6407168 | tf_op jit(solution)/shard_map/dot_general | solution.py:121
  451.2 12.7 %all-reduce.2.cloned.1.call-done = bf16[512,128]{1,0:T(8,128)(2,1)} async-done(((bf16[512,128]{1,0:T(8,128)(2,1)}), bf16[512,128]{1,0:T(8,128)(2,1)}) %all-reduce.2.cloned.1.call-update) | async-done | bytes 131088 | tf_op jit(solution)/shard_map/psum | solution.py:137
  463.9 0.9 convert_element_type.59
  464.8 1.7 gather_fusion.8
  466.5 1.1 broadcast_select_fusion.8
  467.6 6.8 %all-to-all-start.2 = ((f32[16,40,128]{2,1,0:T(8,128)}), f32[16,40,128]{2,1,0:T(8,128)S(1)}, u32[]{:S(2)}, u32[]{:S(2)}) async-start(f32[16,40,128]{2,1,0:T(8,128)} %get-tuple-element.45), calls=%async_computation.3 | async-start | bytes 655360 | tf_op jit(solution)/shard_map/all_to_all | solution.py:147
  474.4 0.6 fusion.31
  475.0 3.9 gather_fusion.6
  478.9 0.3 convert_reduce_fusion
  479.2 7.4 %all-to-all-done.2 = f32[16,40,128]{2,1,0:T(8,128)S(1)} async-done(((f32[16,40,128]{2,1,0:T(8,128)}), f32[16,40,128]{2,1,0:T(8,128)S(1)}, u32[]{:S(2)}, u32[]{:S(2)}) %all-to-all-start.2) | async-done | bytes 327712 | tf_op jit(solution)/shard_map/all_to_all | solution.py:147
  486.6 3.8 all-to-all-start
  491.7 45.5 %gather_fusion.1 = s32[8192]{0:T(1024)S(1)} fusion(s32[6144]{0:T(1024)S(1)} %scatter_custom_fusion.1, s32[8192]{0:T(1024)S(1)} %copy-done.11), kind=kCustom, calls=%fused_computation.3 | custom fusion | bytes 98304 | tf_op jit(solution)/shard_map/gather | solution.py:71
  537.3 1.0 compare_reduce_fusion.19
  538.3 6.3 %fusion.22 = s32[8192]{0:T(1024)S(1)} fusion(pred[8192]{0:T(1024)(128)(4,1)S(1)} %get-tuple-element.25, pred[8192]{0:T(1024)(128)(4,1)S(1)} %get-tuple-element.24, pred[8192]{0:T(1024)(128)(4,1)S(1)} %get-tuple-element.23, pred[8192]{0:T(1024)(128)(4,1)S(1)} %get-tuple-element.22, pred[8192]{0:T(1024)(128)(4,1)S(1)} %get-tuple-element.21, ...), kind=kLoop, calls=%fused_computation.141 | loop fusion | flops 139264 | bytes 213032 | tf_op jit(solution)/shard_map/gather | solution.py:139
  544.6 6.7 %all-to-all-start.1 = ((f32[16,40,128]{2,1,0:T(8,128)}), f32[16,40,128]{2,1,0:T(8,128)S(1)}, u32[]{:S(2)}, u32[]{:S(2)}) async-start(f32[16,40,128]{2,1,0:T(8,128)} %get-tuple-element.44), calls=%async_computation.2 | async-start | bytes 655360 | tf_op jit(solution)/shard_map/all_to_all | solution.py:141
  551.3 10.3 %fusion.11 = bf16[256,128]{1,0:T(8,128)(2,1)} fusion(bf16[8192,256]{1,0:T(8,128)(2,1)} %gather_fusion.12, pred[8192]{0:T(1024)(128)(4,1)S(1)} %get-tuple-element.37, bf16[8192,128]{1,0:T(8,128)(2,1)} %all-gather.4.cloned.1.call-done, pred[8192]{0:T(1024)(128)(4,1)S(1)} %fusion.25), kind=kOutput, calls=%fused_computation.36 | convolution fusion | flops 540049408 | bytes 6373376 | tf_op jit(solution)/shard_map/dot_general | solution.py:120
  561.5 1.4 reshape.582
  563.1 45.5 %gather_fusion.2 = f32[8192]{0:T(1024)S(1)} fusion(f32[8192]{0:T(1024)S(1)} %reduce_sum.64, s32[8192]{0:T(1024)S(1)} %fusion.22), kind=kCustom, calls=%fused_computation.4 | custom fusion | bytes 98304 | tf_op jit(solution)/shard_map/gather | solution.py:139
  608.6 0.6 fusion.23
  609.2 1.7 gather_fusion.11
  610.9 1.7 gather_fusion.7
  612.6 1.7 gather_fusion.9
  614.2 1.3 add_divide_fusion
  (83 shorter events, 2.1 us)
Async XLA Ops:
  7.2 287.6 %copy-start = (f32[512,128]{1,0:T(8,128)S(1)}, f32[512,128]{1,0:T(8,128)}, u32[]{:S(2)}) copy-start(f32[512,128]{1,0:T(8,128)} %param.18) | copy-start | bytes 786436
  7.2 16.7 %copy-start.3 = (s32[8192]{0:T(1024)S(1)}, s32[8192]{0:T(1024)}, u32[]{:S(2)}) copy-start(s32[8192]{0:T(1024)} %param.16) | copy-start | bytes 98308
  7.2 434.3 %reduce-scatter.2.cloned.1.call-start = ((), (), s32[]{:S(2)}) async-start(), calls=%async_computation.5 | async-start | bytes 4456448 | tf_op jit(solution)/shard_map/reduce_scatter | solution.py:129
  20.6 54.9 %copy-start.6 = (s32[8192]{0:T(1024)}, s32[8192]{0:T(1024)S(1)}, u32[]{:S(2)}) copy-start(s32[8192]{0:T(1024)S(1)} %broadcast_clamp_fusion.3) | copy-start | bytes 98308
  72.0 0.6 copy-start.13
  115.9 0.8 copy-start.8
  115.9 1.5 copy-start.7
  115.9 327.3 %all-gather.4.cloned.1.call-start = ((), (), s32[]{:S(2)}) async-start(), calls=%async_computation.4 | async-start | bytes 2228224 | tf_op jit(solution)/shard_map/all_gather | solution.py:117
  116.7 347.2 %all-reduce.2.cloned.1.call-start = ((), (), s32[]{:S(2)}) async-start(), calls=%async_computation.6 | async-start | bytes 262144 | tf_op jit(solution)/shard_map/psum | solution.py:137
  118.3 0.6 copy-start.5
  133.1 3.0 copy-start.2
  259.9 36.6 %copy-start.1 = (f32[512,128]{1,0:T(8,128)S(1)}, f32[512,128]{1,0:T(8,128)}, u32[]{:S(2)}) copy-start(f32[512,128]{1,0:T(8,128)} %param.19) | copy-start | bytes 786436
  383.8 51.3 %copy-start.10 = (s32[8192,1]{0,1:T(1,128)S(1)}, s32[8192,1]{0,1:T(1,128)}, u32[]{:S(2)}) copy-start(s32[8192,1]{0,1:T(1,128)} %get-tuple-element.82) | copy-start | bytes 98308
  383.8 59.4 %copy-start.12 = (bf16[256,128]{1,0:T(8,128)(2,1)S(1)}, bf16[256,128]{1,0:T(8,128)(2,1)}, u32[]{:S(2)}) copy-start(bf16[256,128]{1,0:T(8,128)(2,1)} %param.12) | copy-start | bytes 196612
  383.8 59.4 %copy-start.14 = (f32[256]{0:T(256)S(1)}, f32[256]{0:T(256)}, u32[]{:S(2)}) copy-start(f32[256]{0:T(256)} %copy-done.13) | copy-start | bytes 3076
  443.1 118.4 %all-gather.6.cloned.1.call-start = ((), (), s32[]{:S(2)}) async-start(), calls=%async_computation.7 | async-start | bytes 1081344 | tf_op jit(solution)/shard_map/all_gather | solution.py:138
  466.5 25.2 %copy-start.11 = (s32[8192]{0:T(1024)S(1)}, s32[8192]{0:T(1024)}, u32[]{:S(2)}) copy-start(s32[8192]{0:T(1024)} %get-tuple-element.41) | copy-start | bytes 98308
  467.6 19.1 %all-to-all-start.2 = ((f32[16,40,128]{2,1,0:T(8,128)}), f32[16,40,128]{2,1,0:T(8,128)S(1)}, u32[]{:S(2)}, u32[]{:S(2)}) async-start(f32[16,40,128]{2,1,0:T(8,128)} %get-tuple-element.45), calls=%async_computation.3 | async-start | bytes 655360 | tf_op jit(solution)/shard_map/all_to_all | solution.py:147
  486.6 58.0 %all-to-all-start = ((f32[16,40,128]{2,1,0:T(8,128)}), f32[16,40,128]{2,1,0:T(8,128)S(1)}, u32[]{:S(2)}, u32[]{:S(2)}) async-start(f32[16,40,128]{2,1,0:T(8,128)} %get-tuple-element.43), calls=%async_computation | async-start | bytes 655360 | tf_op jit(solution)/shard_map/all_to_all | solution.py:144
  491.7 46.6 %copy-start.4 = (s32[8192]{0:T(1024)S(1)}, s32[8192]{0:T(1024)}, u32[]{:S(2)}) copy-start(s32[8192]{0:T(1024)} %param.16) | copy-start | bytes 98308
  491.7 46.6 %copy-start.9 = (s32[8192,1]{0,1:T(1,128)S(1)}, s32[8192,1]{0,1:T(1,128)}, u32[]{:S(2)}) copy-start(s32[8192,1]{0,1:T(1,128)} %get-tuple-element.35) | copy-start | bytes 98308
  544.6 68.0 %all-to-all-start.1 = ((f32[16,40,128]{2,1,0:T(8,128)}), f32[16,40,128]{2,1,0:T(8,128)S(1)}, u32[]{:S(2)}, u32[]{:S(2)}) async-start(f32[16,40,128]{2,1,0:T(8,128)} %get-tuple-element.44), calls=%async_computation.2 | async-start | bytes 655360 | tf_op jit(solution)/shard_map/all_to_all | solution.py:141
Sparse Core Ops, SparseCore 0:
  116.0 97.8 reduce-scatter.1
  216.7 60.2 all-gather.3
  443.2 20.5 all-reduce.1
  466.6 55.9 all-gather.5
